TPU v7x, 256 devices: a whole 4x4x8 slice. The times are simulated.
256 devices in a mesh: dom: 32 (over x, z), load: 8 (over y, core).
Axes of the slice: x: 4, y: 4, z: 8, core: 2. Of those that a mesh axis runs over, the one named last changes fastest.
Arguments:
- load_current: float32 [8, 49152], P('load', 'dom'), may hold values from 0.1 to 1
- worst_node: int32 [8], P('load'), may hold values from 0 to 49151
- cond_diag: float32 [49152], P('dom'), may hold values from 0.5 to 4
- branch: float32 [384, 128, 128], P('dom'), may hold values from -0.5 to 0.5
- precond_factor: float32 [384, 128, 128], P('dom'), may hold values from -0.5 to 0.5
- coupling: float32 [5, 384, 128, 128], P(None, 'dom'), may hold values from -0.5 to 0.5
- sep_map: int32 [5, 384], P(None, 'dom'), may hold values from 0 to 11
- strap_ends: int32 [2, 524288], P(None, 'dom'), may hold values from 0 to 1535
Outputs:
- voltages: float32 [2, 8, 49152], P(None, 'load', 'dom')
- strap_grad: float32 [524288], P('dom')
Inputs may be any that keep to these rules, and one draw needn't show every extreme that they name: `sep_map`: each entry names an interior block of the same partition as the separator block. `strap_ends`: both ends of a strap lie in the partition that holds the strap. `worst_node`: a global node index.
All inputs are finite; a program needn't handle non-finite values.
Results may differ from a plain program's by a relative error of at most 0.00017.
Values sent between devices are 32-bit elements; how exact they have to be, the bound alone decides.
No kernel may reach another device: no remote copies, remote signals or barrier semaphores. Data moves between devices by JAX's collectives and lax.ppermute only.
A program may use at most 128 MiB of HBM per device.

v0:
```python
import math

import jax
import jax.numpy as jnp
from jax import lax
from jax.sharding import PartitionSpec as P

ITERS = 4


HIGHEST = lax.Precision.HIGHEST


def swapped(value, axis, apart):
    mask = 2**apart
    pairs = [(source, source ^ mask) for source in range(lax.axis_size(axis))]
    return lax.ppermute(value, axis, pairs)


def subtree_sums(contrib):
    levels = contrib.shape[0]
    finished = []
    pending = contrib
    for level_no in range(levels):
        pending = pending + swapped(pending, "dom", level_no)
        finished.append(pending[0])
        pending = pending[1:]
    return jnp.stack(finished)


def coarse_part(blocks, coupling, picker, level_weights):
    selected = jnp.einsum("ljb,rbn->lrjn", picker, blocks, precision=HIGHEST)
    contrib = jnp.einsum("ljmn,lrjn->lrjm", coupling, selected, precision=HIGHEST)
    group_sums = subtree_sums(contrib)
    returned = jnp.einsum("ljmn,lrjm->lrjn", coupling, group_sums, precision=HIGHEST)
    weighted = picker * level_weights[:, None, None]
    return jnp.einsum("ljb,lrjn->rbn", weighted, returned, precision=HIGHEST)


def factor_apply(factor, blocks):
    inner = jnp.einsum("jnk,rjn->rjk", factor, blocks, precision=HIGHEST)
    return jnp.einsum("jnk,rjk->rjn", factor, inner, precision=HIGHEST)


def column_sums(first, second):
    return lax.psum(jnp.sum(first * second, axis=(1, 2)), "dom")


def shards(
    load_current, worst_node, cond_diag, branch, precond_factor, coupling, sep_map, strap_ends
):
    levels = coupling.shape[0]
    nblocks = branch.shape[0]
    width = branch.shape[1]
    node_count = nblocks * width
    time_count = load_current.shape[0]
    shunt = cond_diag.reshape(nblocks, width)
    picker = (sep_map[:, :, None] == jnp.arange(nblocks, dtype=jnp.int32)[None, None, :]).astype(
        jnp.float32
    )
    op_weights = jnp.array(
        [1.0 / math.sqrt(2.0 ** (level_no + 1)) for level_no in range(levels)], jnp.float32
    )
    pre_weights = 0.5 * op_weights
    node_ids = lax.axis_index("dom") * node_count + jnp.arange(node_count, dtype=jnp.int32)
    adjoint_rhs = (node_ids[None, :] == worst_node[:, None]).astype(jnp.float32)
    sources = jnp.concatenate([load_current, adjoint_rhs], 0).reshape(
        2 * time_count, nblocks, width
    )

    def apply_precond(blocks):
        return (
            blocks / (shunt + 1.0)
            + 0.25 * factor_apply(precond_factor, blocks)
            + coarse_part(blocks, coupling, picker, pre_weights)
        )

    solution = jnp.zeros_like(sources)
    residual = sources
    precond_res = apply_precond(residual)
    rho_now = column_sums(residual, precond_res)
    direction = precond_res
    for iteration in range(ITERS):
        mapped = (
            shunt * direction
            + factor_apply(branch, direction)
            + coarse_part(direction, coupling, picker, op_weights)
        )
        step_size = rho_now / column_sums(direction, mapped)
        solution = solution + step_size[:, None, None] * direction
        residual = residual - step_size[:, None, None] * mapped
        if iteration + 1 < ITERS:
            precond_res = apply_precond(residual)
            rho_new = column_sums(residual, precond_res)
            direction = precond_res + (rho_new / rho_now)[:, None, None] * direction
            rho_now = rho_new
    voltages = solution.reshape(2, time_count, node_count)
    forward = voltages[0]
    adjoint = voltages[1]
    drop_diff = forward[:, strap_ends[0]] - forward[:, strap_ends[1]]
    adj_diff = adjoint[:, strap_ends[0]] - adjoint[:, strap_ends[1]]
    strap_grad = lax.psum(-jnp.sum(adj_diff * drop_diff, axis=0), "load")
    return (voltages, strap_grad)


def solution(mesh):
    placed = (
        P("load", "dom"),
        P("load"),
        P("dom"),
        P("dom", None, None),
        P("dom", None, None),
        P(None, "dom", None, None),
        P(None, "dom"),
        P(None, "dom"),
    )
    return jax.shard_map(
        shards,
        mesh=mesh,
        in_specs=placed,
        out_specs=(P(None, "load", "dom"), P("dom")),
        check_vma=False,
    )
```

profile of v0, /device:TPU:32, one launch (start us, length us, event | category | flops | bytes accessed | tf_op | source)
XLA Modules:
  0.0 1264.0 jit_solution(7190926894018627140)
XLA Ops:
  10.0 7.9 convolution_bitcast_fusion.7
  22.2 3.4 collective-permute-start.1
  27.7 6.0 collective-permute-start.2
  39.7 3.7 collective-permute-start.4
  45.5 3.4 fusion.144
  50.9 6.2 convolution_bitcast_fusion.6
  61.6 2.7 collective-permute-start.6
  64.4 2.9 collective-permute-done.6
  67.4 5.5 collective-permute-start.7
  76.7 2.6 collective-permute-done.8
  79.3 3.1 collective-permute-start.9
  84.8 3.4 fusion.145
  90.0 72.4 %all-reduce = (f32[2]{0:T(128)S(1)}, f32[2]{0:T(128)S(1)}) all-reduce(f32[2]{0:T(128)S(1)} %get-tuple-element.7, f32[2]{0:T(128)S(1)} %get-tuple-element.6), channel_id=1, replica_groups=mesh['dom'=32,'load'=8] {'dom'}, use_global_device_ids=true, to_apply=%region_1.0 | all-reduce | flops 4 | bytes 32 | tf_op jit(solution)/shard_map/psum | solution.py:46
  162.7 8.0 convolution_bitcast_fusion.5
  170.8 4.5 collective-permute-start.10
  177.6 5.0 collective-permute-done.11
  182.8 8.1 collective-permute-done.12
  191.0 3.8 collective-permute-done.13
  195.9 4.4 collective-permute-done.14
  200.4 3.4 fusion.146
  205.6 71.4 %psum.65 = f32[2]{0:T(128)S(1)} all-reduce(f32[2]{0:T(128)S(1)} %get-tuple-element.29), channel_id=1, replica_groups=mesh['dom'=32,'load'=8] {'dom'}, use_global_device_ids=true, to_apply=%region_5.0 | all-reduce | flops 2 | bytes 16 | tf_op jit(solution)/shard_map/psum | solution.py:46
  277.3 8.0 convolution_bitcast_fusion.4
  285.6 4.0 collective-permute-done.15
  289.8 5.0 collective-permute-done.16
  294.9 8.1 collective-permute-done.17
  303.2 3.8 collective-permute-done.18
  308.3 4.4 collective-permute-done.19
  312.7 3.4 fusion.147
  317.9 69.7 %psum.66 = f32[2]{0:T(128)S(1)} all-reduce(f32[2]{0:T(128)S(1)} %get-tuple-element.31), channel_id=1, replica_groups=mesh['dom'=32,'load'=8] {'dom'}, use_global_device_ids=true, to_apply=%region_7.0 | all-reduce | flops 2 | bytes 16 | tf_op jit(solution)/shard_map/psum | solution.py:46
  387.9 8.0 convolution_bitcast_fusion.3
  400.4 5.0 collective-permute-done.21
  405.5 8.1 collective-permute-done.22
  413.7 3.8 collective-permute-done.23
  418.6 4.4 collective-permute-done.24
  423.1 3.4 fusion.148
  428.3 71.4 %psum.67 = f32[2]{0:T(128)S(1)} all-reduce(f32[2]{0:T(128)S(1)} %get-tuple-element.33), channel_id=1, replica_groups=mesh['dom'=32,'load'=8] {'dom'}, use_global_device_ids=true, to_apply=%region_9.0 | all-reduce | flops 2 | bytes 16 | tf_op jit(solution)/shard_map/psum | solution.py:46
  500.0 8.0 convolution_bitcast_fusion.2
  508.3 4.0 collective-permute-done.25
  512.5 5.4 collective-permute-done.26
  518.0 8.0 collective-permute-done.27
  526.1 3.8 collective-permute-done.28
  531.0 4.4 collective-permute-done.29
  535.5 3.4 fusion.149
  540.7 69.3 %psum.68 = f32[2]{0:T(128)S(1)} all-reduce(f32[2]{0:T(128)S(1)} %get-tuple-element.35), channel_id=1, replica_groups=mesh['dom'=32,'load'=8] {'dom'}, use_global_device_ids=true, to_apply=%region_11.0 | all-reduce | flops 2 | bytes 16 | tf_op jit(solution)/shard_map/psum | solution.py:46
  610.3 8.0 convolution_bitcast_fusion.1
  623.1 5.0 collective-permute-done.31
  628.2 8.1 collective-permute-done.32
  636.5 3.8 collective-permute-done.33
  641.6 4.4 collective-permute-done.34
  646.0 3.4 fusion.150
  651.2 71.5 %psum.69 = f32[2]{0:T(128)S(1)} all-reduce(f32[2]{0:T(128)S(1)} %get-tuple-element.37), channel_id=1, replica_groups=mesh['dom'=32,'load'=8] {'dom'}, use_global_device_ids=true, to_apply=%region_13.0 | all-reduce | flops 2 | bytes 16 | tf_op jit(solution)/shard_map/psum | solution.py:46
  723.0 8.0 convolution_bitcast_fusion
  731.4 3.9 collective-permute-done.35
  735.5 5.0 collective-permute-done.36
  740.6 8.1 collective-permute-done.37
  748.8 3.8 collective-permute-done.38
  753.7 4.4 collective-permute-done.39
  758.1 3.4 fusion.151
  763.4 69.6 %psum.70 = f32[2]{0:T(128)S(1)} all-reduce(f32[2]{0:T(128)S(1)} %fusion.21), channel_id=1, replica_groups=mesh['dom'=32,'load'=8] {'dom'}, use_global_device_ids=true, to_apply=%region_15.0 | all-reduce | flops 2 | bytes 16 | tf_op jit(solution)/shard_map/psum | solution.py:46
  833.1 90.5 %gather_fusion.3 = f32[16384]{0:T(1024)S(1)} fusion(f32[1536]{0:T(1024)S(1)} %bitcast.279, s32[16384]{0:T(1024)S(1)} %get-tuple-element.39), kind=kCustom, calls=%fused_computation.3 | custom fusion | bytes 196608 | tf_op jit(solution)/shard_map/gather | solution.py:100
  923.6 90.5 %gather_fusion.1 = f32[16384]{0:T(1024)S(1)} fusion(f32[1536]{0:T(1024)S(1)} %bitcast.281, s32[16384]{0:T(1024)S(1)} %get-tuple-element.39), kind=kCustom, calls=%fused_computation.1 | custom fusion | bytes 196608 | tf_op jit(solution)/shard_map/gather | solution.py:101
  1014.2 90.5 %gather_fusion = f32[16384]{0:T(1024)S(1)} fusion(f32[1536]{0:T(1024)S(1)} %bitcast.282, s32[16384]{0:T(1024)S(1)} %get-tuple-element.40), kind=kCustom, calls=%fused_computation | custom fusion | bytes 196608 | tf_op jit(solution)/shard_map/gather | solution.py:101
  1104.7 90.5 %gather_fusion.2 = f32[16384]{0:T(1024)S(1)} fusion(f32[1536]{0:T(1024)S(1)} %bitcast.280, s32[16384]{0:T(1024)S(1)} %get-tuple-element.40), kind=kCustom, calls=%fused_computation.2 | custom fusion | bytes 196608 | tf_op jit(solution)/shard_map/gather | solution.py:100
  1196.5 58.9 %all-reduce.3.cloned.1.call-done = f32[16384]{0:T(1024)} async-done(((f32[16384]{0:T(1024)}), f32[16384]{0:T(1024)}) %all-reduce.3.cloned.1.call-update) | async-done | bytes 65552 | tf_op jit(solution)/shard_map/psum | solution.py:102
  (227 shorter events, 68.0 us)
Async XLA Ops:
  7.2 12.6 copy-start
  7.2 12.6 copy-start.10
  7.2 36.1 %copy-start.11 = (f32[1536]{0:T(1024)S(1)}, f32[1536]{0:T(1024)}, u32[]{:S(2)}) copy-start(f32[1536]{0:T(1024)} %param.11) | copy-start | bytes 18436
  7.2 1248.3 %all-reduce.3.cloned.1.call-start = ((), (), s32[]{:S(2)}) async-start(), calls=%async_computation | async-start | bytes 131072 | tf_op jit(solution)/shard_map/psum | solution.py:102
  8.0 37.6 %copy-start.1 = (f32[5,12,128,128]{3,2,1,0:T(8,128)S(1)}, f32[5,12,128,128]{3,2,1,0:T(8,128)}, u32[]{:S(2)}) copy-start(f32[5,12,128,128]{3,2,1,0:T(8,128)} %param.14) | copy-start | bytes 11796484
  10.0 39.0 %copy-start.9 = (s32[5,12]{1,0:T(8,128)S(1)}, s32[5,12]{1,0:T(8,128)}, u32[]{:S(2)}) copy-start(s32[5,12]{1,0:T(8,128)} %param.15) | copy-start | bytes 724
  10.0 39.0 %copy-start.14 = (f32[5]{0:T(128)S(1)}, f32[5]{0:T(128)}, u32[]{:S(2)}) copy-start(f32[5]{0:T(128)} %constant.32) | copy-start | bytes 64
  17.9 4.3 collective-permute-start
  22.2 5.5 collective-permute-start.1
  27.7 8.0 collective-permute-start.2
  35.7 3.9 collective-permute-start.3
  39.7 5.8 collective-permute-start.4
  49.0 33.4 %copy-start.8 = (f32[12,128,128]{2,1,0:T(8,128)S(1)}, f32[12,128,128]{2,1,0:T(8,128)}, u32[]{:S(2)}) copy-start(f32[12,128,128]{2,1,0:T(8,128)} %param.12) | copy-start | bytes 2359300
  50.9 37.3 %copy-start.13 = (f32[5]{0:T(128)S(1)}, f32[5]{0:T(128)}, u32[]{:S(2)}) copy-start(f32[5]{0:T(128)} %constant.25.clone) | copy-start | bytes 64
  57.1 4.5 collective-permute-start.5
  61.6 5.7 collective-permute-start.6
  67.4 8.0 collective-permute-start.7
  75.3 3.9 collective-permute-start.8
  79.3 5.5 collective-permute-start.9
  162.4 37.9 %copy-start.2 = (f32[5,12,128,128]{3,2,1,0:T(8,128)S(1)}, f32[5,12,128,128]{3,2,1,0:T(8,128)}, u32[]{:S(2)}) copy-start(f32[5,12,128,128]{3,2,1,0:T(8,128)} %param.14) | copy-start | bytes 11796484
  170.8 6.7 collective-permute-start.10
  177.5 5.1 collective-permute-start.11
  182.6 8.2 collective-permute-start.12
  190.9 3.9 collective-permute-start.13
  194.8 5.5 collective-permute-start.14
  276.9 35.8 %copy-start.3 = (f32[5,12,128,128]{3,2,1,0:T(8,128)S(1)}, f32[5,12,128,128]{3,2,1,0:T(8,128)}, u32[]{:S(2)}) copy-start(f32[5,12,128,128]{3,2,1,0:T(8,128)} %param.14) | copy-start | bytes 11796484
  285.3 4.3 collective-permute-start.15
  289.7 5.1 collective-permute-start.16
  294.8 8.2 collective-permute-start.17
  303.1 3.9 collective-permute-start.18
  307.0 5.7 collective-permute-start.19
  387.6 35.5 %copy-start.4 = (f32[5,12,128,128]{3,2,1,0:T(8,128)S(1)}, f32[5,12,128,128]{3,2,1,0:T(8,128)}, u32[]{:S(2)}) copy-start(f32[5,12,128,128]{3,2,1,0:T(8,128)} %param.14) | copy-start | bytes 11796484
  396.0 4.3 collective-permute-start.20
  400.3 5.1 collective-permute-start.21
  405.4 8.2 collective-permute-start.22
  413.6 3.9 collective-permute-start.23
  417.6 5.5 collective-permute-start.24
  499.7 35.8 %copy-start.5 = (f32[5,12,128,128]{3,2,1,0:T(8,128)S(1)}, f32[5,12,128,128]{3,2,1,0:T(8,128)}, u32[]{:S(2)}) copy-start(f32[5,12,128,128]{3,2,1,0:T(8,128)} %param.14) | copy-start | bytes 11796484
  508.0 4.3 collective-permute-start.25
  512.3 5.5 collective-permute-start.26
  517.9 8.1 collective-permute-start.27
  526.0 3.9 collective-permute-start.28
  530.0 5.5 collective-permute-start.29
  610.0 36.0 %copy-start.6 = (f32[5,12,128,128]{3,2,1,0:T(8,128)S(1)}, f32[5,12,128,128]{3,2,1,0:T(8,128)}, u32[]{:S(2)}) copy-start(f32[5,12,128,128]{3,2,1,0:T(8,128)} %param.14) | copy-start | bytes 11796484
  618.4 4.6 collective-permute-start.30
  623.0 5.1 collective-permute-start.31
  628.1 8.2 collective-permute-start.32
  636.3 3.9 collective-permute-start.33
  640.3 5.7 collective-permute-start.34
  646.0 85.3 %copy-start.12 = (s32[2,16384]{1,0:T(2,128)S(1)}, s32[2,16384]{1,0:T(2,128)}, u32[]{:S(2)}) copy-start(s32[2,16384]{1,0:T(2,128)} %param.16) | copy-start | bytes 393220
  722.7 35.5 %copy-start.7 = (f32[5,12,128,128]{3,2,1,0:T(8,128)S(1)}, f32[5,12,128,128]{3,2,1,0:T(8,128)}, u32[]{:S(2)}) copy-start(f32[5,12,128,128]{3,2,1,0:T(8,128)} %param.14) | copy-start | bytes 11796484
  731.0 4.3 collective-permute-start.35
  735.4 5.1 collective-permute-start.36
  740.5 8.2 collective-permute-start.37
  748.7 3.9 collective-permute-start.38
  752.6 5.5 collective-permute-start.39
Sparse Core Ops, SparseCore 0:
  1196.1 59.3 all-reduce.2
where the time goes:
time: 1270 us; the launch traced here: 1260 us
  blocking collectives  495 us (39%)
  local copies, waits for them, and re-layouts  365 us (29%)
  waiting for transfers between devices  227 us (18%)
  matrix products  113 us (9%)
  starting transfers between devices  45.1 us (4%)
  between operations  15.9 us (1%)
    psum x7, blocking collectives, column_sums(): return lax.psum(jnp.sum(first * second, axis=(1, 2)), 'dom')  495 us
    gather x2, local copies, waits for them, and re-layouts, shards(): drop_diff = forward[:, strap_ends[0]] - forward[:, strap_ends[1]]  181 us
    gather x2, local copies, waits for them, and re-layouts, shards(): adj_diff = adjoint[:, strap_ends[0]] - adjoint[:, strap_ends[1]]  181 us
    ppermute x40, waiting for transfers between devices, swapped(): return lax.ppermute(value, axis, pairs)  168 us
    dot_general x8, matrix products, coarse_part(): jnp.einsum('ljmn,lrjn->lrjm', coupling, selected, precision=HIGHEST)  62.3 us
    psum x1, waiting for transfers between devices, shards(): strap_grad = lax.psum(-jnp.sum(adj_diff * drop_diff, axis=0), 'load')  58.9 us
    ppermute x40, starting transfers between devices, swapped(): return lax.ppermute(value, axis, pairs)  45 us
    dot_general x8, matrix products, coarse_part(): jnp.einsum('ljmn,lrjm->lrjn', coupling, group_sums, precision=HIGHEST)  27.5 us
  transfers between devices with their start and end apart: 41, of which 41 were waited for; matrix products, arithmetic and copies ran while one was open for 1% of the time, Pallas kernels for 0%

commit v1 on v0

v1 whole, which is shorter than its diff:
```python
import math

import jax
import jax.numpy as jnp
from jax import lax
from jax.experimental import pallas as pl
from jax.experimental.pallas import tpu as pltpu
from jax.sharding import PartitionSpec as P

ITERS = 4
LEVELS = 5
NB = 12
W = 128
ROWS = 2 * NB
OP = [1.0 / math.sqrt(2.0 ** (level + 1)) for level in range(LEVELS)]
PRE = [0.5 * c for c in OP]
F32 = jnp.float32
BF16 = jnp.bfloat16
VMEM = pl.BlockSpec(memory_space=pltpu.VMEM)
SMEM = pl.BlockSpec(memory_space=pltpu.SMEM)
PARAMS = pltpu.CompilerParams(vmem_limit_bytes=40 * 1024 * 1024)


def split_rows(tile):
    high = tile.astype(BF16).astype(F32)
    return jnp.concatenate([high, tile - high], axis=0).astype(BF16)


def times(rows, matrix):
    out = lax.dot_general(
        jnp.concatenate([rows, rows], axis=1),
        matrix,
        (((1,), (0,)), ((), ())),
        preferred_element_type=F32,
    )
    return out[:8] + out[8:]


def times_t(rows, matrix):
    out = lax.dot_general(rows, matrix, (((1,), (1,)), ((), ())), preferred_element_type=F32)
    out = out[:8] + out[8:]
    return out[:, :W] + out[:, W:]


def split_kernel(mat_ref, out_ref):
    mats = mat_ref[...]
    high = mats.astype(BF16)
    out_ref[:, :W, :] = high
    out_ref[:, W:, :] = (mats - high.astype(F32)).astype(BF16)


def split_matrices(mats):
    count = mats.shape[0]
    step = 12
    return pl.pallas_call(
        split_kernel,
        grid=(count // step,),
        in_specs=[pl.BlockSpec((step, W, W), lambda i: (i, 0, 0))],
        out_specs=pl.BlockSpec((step, 2 * W, W), lambda i: (i, 0, 0)),
        out_shape=jax.ShapeDtypeStruct((count, 2 * W, W), BF16),
        compiler_params=PARAMS,
        name="split_matrices",
    )(mats)


def side_totals(square):
    total = square[0:8] + square[8:16] + square[16:24]
    total = total + pltpu.roll(total, 2, 0)
    total = total + pltpu.roll(total, 4, 0)
    return jnp.broadcast_to(jnp.sum(total, axis=1, keepdims=True), (8, W))


def coarse_back(sums, weights, coupling, sep, part, acc):
    for level in range(LEVELS):
        for group in range(NB // 4):
            rows = split_rows(sums[level][8 * group : 8 * group + 8, :] * weights[level])
            for member in range(4):
                j = 4 * group + member
                out = times(rows, coupling[level * NB + j])
                part[level * NB + j] = out if member == 0 else pltpu.roll(out, 8 - 2 * member, 0)
    acc[...] = jnp.zeros((NB, 8, W), F32)
    for level in range(LEVELS):
        for j in range(NB):
            k = sep[level, j]
            acc[k] = acc[k] + part[level * NB + j]


def local_part(vec, diag, scale, factor, coupling, sep, split, payload, applied):
    for k in range(NB):
        split[k] = split_rows(vec[k])
    for level in range(LEVELS):
        for j in range(NB):
            out = times_t(split[sep[level, j]], coupling[level * NB + j])
            payload[level * ROWS + 2 * j : level * ROWS + 2 * j + 2, :] = out[0:2]
    for k in range(NB):
        inner = times(split[k], factor[k])
        scaled = diag[k] * vec[k]
        square = scaled * vec[k] + scale * (inner * inner)
        payload[LEVELS * ROWS + 2 * k : LEVELS * ROWS + 2 * k + 2, :] = square[0:2]
        applied[k] = scaled + scale * times_t(split_rows(inner), factor[k])


def first_kernel(sep, vec, shunt, factor, coupling, payload, applied, split):
    v = [vec[k] for k in range(NB)]
    d = [1.0 / (shunt[k] + 1.0) for k in range(NB)]
    local_part(v, d, 0.25, factor, coupling, sep, split, payload, applied)


def keep_sides(tile):
    return jnp.where(lax.broadcasted_iota(jnp.int32, (8, W), 0) < 2, tile, 0.0)


def make_precond_kernel(first):
    def kernel(sep, *refs):
        sums = refs[:LEVELS]
        refs = refs[LEVELS:]
        if first:
            square, applied, shunt, factor, coupling, payload, next_applied, direction, rho, split, part, acc = refs
        else:
            (square, applied, shunt, factor, coupling, old_direction, old_rho) = refs[:7]
            payload, next_applied, direction, rho, split, part, acc = refs[7:]
        coarse_back(sums, PRE, coupling, sep, part, acc)
        rho_new = side_totals(square)
        if not first:
            ratio = rho_new / old_rho[...]
        rho[...] = rho_new
        vec = []
        for k in range(NB):
            tile = applied[k] + acc[k]
            if not first:
                tile = tile + ratio * old_direction[k]
            tile = keep_sides(tile)
            direction[k] = tile
            vec.append(tile)
        d = [shunt[k] for k in range(NB)]
        local_part(vec, d, 1.0, factor, coupling, sep, split, payload, next_applied)

    return kernel


def make_operator_kernel(first):
    def kernel(sep, *refs):
        sums = refs[:LEVELS]
        refs = refs[LEVELS:]
        square, applied, shunt, factor, coupling, direction, residual, rho = refs[:8]
        refs = refs[8:]
        if not first:
            estimate = refs[0]
            refs = refs[1:]
        payload, next_applied, next_residual, next_estimate, split, part, acc = refs
        coarse_back(sums, OP, coupling, sep, part, acc)
        step = rho[...] / side_totals(square)
        vec = []
        for k in range(NB):
            gain = step * direction[k]
            next_estimate[k] = gain if first else estimate[k] + gain
            tile = keep_sides(residual[k] - step * (applied[k] + acc[k]))
            next_residual[k] = tile
            vec.append(tile)
        d = [1.0 / (shunt[k] + 1.0) for k in range(NB)]
        local_part(vec, d, 0.25, factor, coupling, sep, split, payload, next_applied)

    return kernel


def last_kernel(square, direction, rho, estimate, ends, volts, terms):
    step = rho[...] / side_totals(square)
    for k in range(NB):
        tile = estimate[k] + step * direction[k]
        volts[0, k : k + 1, :] = tile[0:1]
        volts[1, k : k + 1, :] = tile[1:2]

    def chunk(i, carry):
        def drops(side):
            def at(end):
                index = ends[end, pl.ds(pl.multiple_of(8 * i, 8), 8), :]
                block = index >> 7
                lane = index & (W - 1)
                value = jnp.zeros((8, W), F32)
                for k in range(NB):
                    row = jnp.broadcast_to(volts[side, k : k + 1, :], (8, W))
                    value = jnp.where(block == k, jnp.take_along_axis(row, lane, axis=1), value)
                return value

            return at(0) - at(1)

        terms[pl.ds(pl.multiple_of(8 * i, 8), 8), :] = -(drops(1) * drops(0))
        return carry

    lax.fori_loop(0, terms.shape[0] // 8, chunk, 0)


TILES = jax.ShapeDtypeStruct((NB, 8, W), F32)
PAYLOAD = jax.ShapeDtypeStruct(((LEVELS + 1) * ROWS, W), F32)
TILE = jax.ShapeDtypeStruct((8, W), F32)
SPLIT = pltpu.VMEM((NB, 16, W), BF16)
PART = pltpu.VMEM((LEVELS * NB, 8, W), F32)
ACC = pltpu.VMEM((NB, 8, W), F32)


def call(kernel, name, args, outs, scratch, first_smem=True):
    return pl.pallas_call(
        kernel,
        in_specs=[SMEM if first_smem and i == 0 else VMEM for i in range(len(args))],
        out_specs=[VMEM] * len(outs),
        out_shape=outs,
        scratch_shapes=scratch,
        compiler_params=PARAMS,
        name=name,
    )(*args)


def tree_partners(level, count):
    half = 2**level
    if level == 2:
        inside = {0: 6, 1: 7, 2: 4, 3: 5, 4: 2, 5: 3, 6: 0, 7: 1}
        return [(s, s // 8 * 8 + inside[s % 8]) for s in range(count)]
    if level == 4:
        return [(s, (3 - s // 8) * 8 + s % 8) for s in range(count)]
    return [(s, s ^ half) for s in range(count)]


def tree_exchange(payload, weights):
    count = lax.axis_size("dom")
    pending = payload
    finished = []
    for level in range(LEVELS):
        pending = pending + lax.ppermute(pending, "dom", tree_partners(level, count))
        done = pending[:ROWS]
        finished.append(done)
        square = pending[-ROWS:] + weights[level] * (done * done)
        if level + 1 < LEVELS:
            pending = jnp.concatenate([pending[ROWS:-ROWS], square], axis=0)
    return finished, square


def shards(
    load_current, worst_node, cond_diag, branch, precond_factor, coupling, sep_map, strap_ends
):
    node_count = NB * W
    shunt = jnp.broadcast_to(cond_diag.reshape(NB, 1, W), (NB, 8, W))
    node_ids = lax.axis_index("dom") * node_count + jnp.arange(node_count, dtype=jnp.int32)
    adjoint = (node_ids == worst_node[0]).astype(F32).reshape(NB, 1, W)
    sources = jnp.concatenate(
        [load_current.reshape(NB, 1, W), adjoint, jnp.zeros((NB, 6, W), F32)], axis=1
    )
    ends = strap_ends.reshape(2, -1, W)
    cpl = split_matrices(coupling.reshape(LEVELS * NB, W, W))
    pre = split_matrices(precond_factor)
    brn = split_matrices(branch)

    payload, applied = call(
        first_kernel, "first_part", (sep_map, sources, shunt, pre, cpl), [PAYLOAD, TILES], [SPLIT]
    )
    residual = sources
    direction = rho = estimate = None
    for iteration in range(ITERS):
        first = iteration == 0
        sums, square = tree_exchange(payload, PRE)
        args = (sep_map, *sums, square, applied, shunt, brn, cpl)
        if not first:
            args += (direction, rho)
        payload, applied, direction, rho = call(
            make_precond_kernel(first),
            "precond_round",
            args,
            [PAYLOAD, TILES, TILES, TILE],
            [SPLIT, PART, ACC],
        )
        sums, square = tree_exchange(payload, OP)
        if iteration + 1 < ITERS:
            args = (sep_map, *sums, square, applied, shunt, pre, cpl, direction, residual, rho)
            if not first:
                args += (estimate,)
            payload, applied, residual, estimate = call(
                make_operator_kernel(first),
                "operator_round",
                args,
                [PAYLOAD, TILES, TILES, TILES],
                [SPLIT, PART, ACC],
            )
    volts, terms = call(
        last_kernel,
        "straps",
        (square, direction, rho, estimate, ends),
        [
            jax.ShapeDtypeStruct((2, NB, W), F32),
            jax.ShapeDtypeStruct(ends.shape[1:], F32),
        ],
        [],
        first_smem=False,
    )
    for pairs in (
        [(s, s ^ 1) for s in range(8)],
        [(s, s ^ 2) for s in range(8)],
        [(s, (3 - s // 2) * 2 + s % 2) for s in range(8)],
    ):
        terms = terms + lax.ppermute(terms, "load", pairs)
    return (volts.reshape(2, 1, node_count), terms.reshape(-1))


def solution(mesh):
    placed = (
        P("load", "dom"),
        P("load"),
        P("dom"),
        P("dom", None, None),
        P("dom", None, None),
        P(None, "dom", None, None),
        P(None, "dom"),
        P(None, "dom"),
    )
    return jax.shard_map(
        shards,
        mesh=mesh,
        in_specs=placed,
        out_specs=(P(None, "load", "dom"), P("dom")),
        check_vma=False,
    )
```

time: 1270 us -> 269 us (0.21)
  blocking collectives: 495 us -> 0 us
  local copies, waits for them, and re-layouts: 365 us -> 6.95 us
  matrix products: 113 us -> 0 us
  waiting for transfers between devices: 227 us -> 137 us
  starting transfers between devices: 45.1 us -> 87.4 us
  Pallas kernels: 0 us -> 29 us
  between operations: 15.9 us -> 2.38 us
    psum x7 -> x0, blocking collectives: 495 us -> none  [column_sums(): return lax.psum(jnp.sum(first * second, axis=(1, 2)), 'dom')]
    gather x4 -> x0, local copies, waits for them, and re-layouts: 362 us -> none  [the longest x2 181 us: shards(): drop_diff = forward[:, strap_ends[0]] - forward[:, strap_ends[1]]]
    dot_general x48 -> x0, matrix products: 113 us -> none  [the longest x8 62.3 us: coarse_part(): jnp.einsum('ljmn,lrjn->lrjm', coupling, selected, precision=HIGHEST)]
    psum x1 -> x0, waiting for transfers between devices: 58.9 us -> none  [shards(): strap_grad = lax.psum(-jnp.sum(adj_diff * drop_diff, axis=0), 'load')]
    ppermute x40 -> x43, starting transfers between devices: 45 us -> 87.4 us  [the longest x40 83 us: tree_exchange(): lax.ppermute(pending, 'dom', tree_partners(level, count))]
    ppermute x40 -> x43, waiting for transfers between devices: 168 us -> 137 us  [the longest x40 131 us: tree_exchange(): lax.ppermute(pending, 'dom', tree_partners(level, count))]
    pallas_call x0 -> x12, Pallas kernels: none -> 29 us  [the longest x9 28 us: call(): pl.pallas_call(kernel, in_specs=[SMEM if first_smem and i == 0 else VMEM...]
  transfers between devices with their start and end apart: 41 -> 43, of which waited for: 41 -> 43; matrix products, arithmetic and copies ran while one was open for 1% -> 0% of each run, Pallas kernels for 0% -> 0%
where the time goes in v1:
time: 269 us; the launch traced here: 264 us
  waiting for transfers between devices  137 us (51%)
  starting transfers between devices  87.4 us (32%)
  Pallas kernels  29 us (11%)
  local copies, waits for them, and re-layouts  6.95 us (3%)
    ppermute x40, waiting for transfers between devices, tree_exchange(): lax.ppermute(pending, 'dom', tree_partners(level, count))  131 us
    ppermute x40, starting transfers between devices, tree_exchange(): lax.ppermute(pending, 'dom', tree_partners(level, count))  83 us
    pallas_call x9, Pallas kernels, call(): pl.pallas_call(kernel, in_specs=[SMEM if first_smem and i == 0 else VMEM...  28 us
    ppermute x3, waiting for transfers between devices, shards(): terms = terms + lax.ppermute(terms, 'load', pairs)  6.26 us
    unnamed x21, local copies, waits for them, and re-layouts  6.15 us
  transfers between devices with their start and end apart: 43, of which 43 were waited for; matrix products, arithmetic and copies ran while one was open for 0% of the time, Pallas kernels for 0%

profile of v1, /device:TPU:32, one launch (start us, length us, event | category | flops | bytes accessed | tf_op | source)
XLA Modules:
  0.0 264.4 jit_solution(12586548394862026527)
XLA Ops:
  8.5 2.6 first_part.1
  13.0 2.5 collective-permute-done
  15.5 3.4 %collective-permute-start.1 = (f32[120,128]{1,0:T(8,128)S(1)}, f32[120,128]{1,0:T(8,128)S(1)}, u32[]{:S(2)}, u32[]{:S(2)}) collective-permute-start(f32[120,128]{1,0:T(8,128)S(1)} %pad_maximum_fusion), channel_id=1, source_target_pairs={{0,16},{8,24},{16,0},{24,8},{32,48},{40,56},{48,32},{56,40},{64,80... | collective-permute-start | bytes 184328 | tf_op jit(solution)/shard_map/ppermute | solution.py:228
  21.2 5.7 %collective-permute-start.2 = (f32[96,128]{1,0:T(8,128)S(1)}, f32[96,128]{1,0:T(8,128)S(1)}, u32[]{:S(2)}, u32[]{:S(2)}) collective-permute-start(f32[96,128]{1,0:T(8,128)S(1)} %pad_maximum_fusion.8), channel_id=1, source_target_pairs={{0,48},{8,56},{16,32},{24,40},{32,16},{40,24},{48,0},{56,8},{64,11... | collective-permute-start | bytes 147464 | tf_op jit(solution)/shard_map/ppermute | solution.py:228
  26.9 2.6 collective-permute-done.2
  31.0 2.6 collective-permute-done.3
  33.6 2.8 %collective-permute-start.4 = (f32[48,128]{1,0:T(8,128)S(1)}, f32[48,128]{1,0:T(8,128)S(1)}, u32[]{:S(2)}, u32[]{:S(2)}) collective-permute-start(f32[48,128]{1,0:T(8,128)S(1)} %pad_maximum_fusion.24), channel_id=1, source_target_pairs={{0,192},{8,200},{16,208},{24,216},{32,224},{40,232},{48,240},{56,2... | collective-permute-start | bytes 73736 | tf_op jit(solution)/shard_map/ppermute | solution.py:228
  38.8 3.2 %precond_round.4 = (f32[144,128]{1,0:T(8,128)S(1)}, f32[12,8,128]{2,1,0:T(8,128)S(1)}, f32[12,8,128]{2,1,0:T(8,128)S(1)}, f32[8,128]{1,0:T(8,128)S(1)}) custom-call(s32[5,12]{1,0:T(8,128)S(1)} %copy-done.6, f32[24,128]{1,0:T(8,128)S(1)} %get-tuple-element.79.refs_0_, f32[24,128]{1,0:T(8,128)S(1)} %get-tuple-element.93.refs_1_, ...), custom_call_target="tpu_custom_call" | custom-call | tf_op jit(solution)/shard_map/precond_round/pallas_call | solution.py:202
  42.1 4.3 %collective-permute-done.5 = f32[144,128]{1,0:T(8,128)S(1)} collective-permute-done((f32[144,128]{1,0:T(8,128)S(1)}, f32[144,128]{1,0:T(8,128)S(1)}, u32[]{:S(2)}, u32[]{:S(2)}) %collective-permute-start.5) | collective-permute-done | bytes 73760 | tf_op jit(solution)/shard_map/ppermute | solution.py:228
  47.7 4.0 %collective-permute-done.6 = f32[120,128]{1,0:T(8,128)S(1)} collective-permute-done((f32[120,128]{1,0:T(8,128)S(1)}, f32[120,128]{1,0:T(8,128)S(1)}, u32[]{:S(2)}, u32[]{:S(2)}) %collective-permute-start.6) | collective-permute-done | bytes 61472 | tf_op jit(solution)/shard_map/ppermute | solution.py:228
  51.7 4.3 %collective-permute-start.7 = (f32[96,128]{1,0:T(8,128)S(1)}, f32[96,128]{1,0:T(8,128)S(1)}, u32[]{:S(2)}, u32[]{:S(2)}) collective-permute-start(f32[96,128]{1,0:T(8,128)S(1)} %pad_maximum_fusion.9), channel_id=1, source_target_pairs={{0,48},{8,56},{16,32},{24,40},{32,16},{40,24},{48,0},{56,8},{64,11... | collective-permute-start | bytes 147464 | tf_op jit(solution)/shard_map/ppermute | solution.py:228
  58.5 3.8 %collective-permute-done.8 = f32[72,128]{1,0:T(8,128)S(1)} collective-permute-done((f32[72,128]{1,0:T(8,128)S(1)}, f32[72,128]{1,0:T(8,128)S(1)}, u32[]{:S(2)}, u32[]{:S(2)}) %collective-permute-start.8) | collective-permute-done | bytes 36896 | tf_op jit(solution)/shard_map/ppermute | solution.py:228
  62.3 2.8 %collective-permute-start.9 = (f32[48,128]{1,0:T(8,128)S(1)}, f32[48,128]{1,0:T(8,128)S(1)}, u32[]{:S(2)}, u32[]{:S(2)}) collective-permute-start(f32[48,128]{1,0:T(8,128)S(1)} %pad_maximum_fusion.25), channel_id=1, source_target_pairs={{0,192},{8,200},{16,208},{24,216},{32,224},{40,232},{48,240},{56,2... | collective-permute-start | bytes 73736 | tf_op jit(solution)/shard_map/ppermute | solution.py:228
  65.0 2.4 collective-permute-done.9
  67.4 3.2 %operator_round.3 = (f32[144,128]{1,0:T(8,128)S(1)}, f32[12,8,128]{2,1,0:T(8,128)S(1)}, f32[12,8,128]{2,1,0:T(8,128)S(1)}, f32[12,8,128]{2,1,0:T(8,128)S(1)}) custom-call(s32[5,12]{1,0:T(8,128)S(1)} %copy-done.6, f32[24,128]{1,0:T(8,128)S(1)} %get-tuple-element.77.refs_0_, f32[24,128]{1,0:T(8,128)S(1)} %get-tuple-element.91.refs_1_, ...), custom_call_target="tpu_custom_call" | custom-call | tf_op jit(solution)/shard_map/operator_round/pallas_call | solution.py:202
  70.8 4.3 %collective-permute-done.10 = f32[144,128]{1,0:T(8,128)S(1)} collective-permute-done((f32[144,128]{1,0:T(8,128)S(1)}, f32[144,128]{1,0:T(8,128)S(1)}, u32[]{:S(2)}, u32[]{:S(2)}) %collective-permute-start.10) | collective-permute-done | bytes 73760 | tf_op jit(solution)/shard_map/ppermute | solution.py:228
  76.9 3.5 %collective-permute-done.11 = f32[120,128]{1,0:T(8,128)S(1)} collective-permute-done((f32[120,128]{1,0:T(8,128)S(1)}, f32[120,128]{1,0:T(8,128)S(1)}, u32[]{:S(2)}, u32[]{:S(2)}) %collective-permute-start.11) | collective-permute-done | bytes 61472 | tf_op jit(solution)/shard_map/ppermute | solution.py:228
  80.4 4.5 %collective-permute-start.12 = (f32[96,128]{1,0:T(8,128)S(1)}, f32[96,128]{1,0:T(8,128)S(1)}, u32[]{:S(2)}, u32[]{:S(2)}) collective-permute-start(f32[96,128]{1,0:T(8,128)S(1)} %pad_maximum_fusion.10), channel_id=1, source_target_pairs={{0,48},{8,56},{16,32},{24,40},{32,16},{40,24},{48,0},{56,8},{64,11... | collective-permute-start | bytes 147464 | tf_op jit(solution)/shard_map/ppermute | solution.py:228
  84.9 2.6 collective-permute-done.12
  87.6 3.9 %collective-permute-done.13 = f32[72,128]{1,0:T(8,128)S(1)} collective-permute-done((f32[72,128]{1,0:T(8,128)S(1)}, f32[72,128]{1,0:T(8,128)S(1)}, u32[]{:S(2)}, u32[]{:S(2)}) %collective-permute-start.13) | collective-permute-done | bytes 36896 | tf_op jit(solution)/shard_map/ppermute | solution.py:228
  91.6 2.7 %collective-permute-start.14 = (f32[48,128]{1,0:T(8,128)S(1)}, f32[48,128]{1,0:T(8,128)S(1)}, u32[]{:S(2)}, u32[]{:S(2)}) collective-permute-start(f32[48,128]{1,0:T(8,128)S(1)} %pad_maximum_fusion.26), channel_id=1, source_target_pairs={{0,192},{8,200},{16,208},{24,216},{32,224},{40,232},{48,240},{56,2... | collective-permute-start | bytes 73736 | tf_op jit(solution)/shard_map/ppermute | solution.py:228
  94.3 2.5 collective-permute-done.14
  96.8 3.2 %precond_round.5 = (f32[144,128]{1,0:T(8,128)S(1)}, f32[12,8,128]{2,1,0:T(8,128)S(1)}, f32[12,8,128]{2,1,0:T(8,128)S(1)}, f32[8,128]{1,0:T(8,128)S(1)}) custom-call(s32[5,12]{1,0:T(8,128)S(1)} %copy-done.6, f32[24,128]{1,0:T(8,128)S(1)} %get-tuple-element.75.refs_0_, f32[24,128]{1,0:T(8,128)S(1)} %get-tuple-element.89.refs_1_, ...), custom_call_target="tpu_custom_call" | custom-call | tf_op jit(solution)/shard_map/precond_round/pallas_call | solution.py:202
  100.1 4.3 %collective-permute-done.15 = f32[144,128]{1,0:T(8,128)S(1)} collective-permute-done((f32[144,128]{1,0:T(8,128)S(1)}, f32[144,128]{1,0:T(8,128)S(1)}, u32[]{:S(2)}, u32[]{:S(2)}) %collective-permute-start.15) | collective-permute-done | bytes 73760 | tf_op jit(solution)/shard_map/ppermute | solution.py:228
  106.3 3.4 %collective-permute-done.16 = f32[120,128]{1,0:T(8,128)S(1)} collective-permute-done((f32[120,128]{1,0:T(8,128)S(1)}, f32[120,128]{1,0:T(8,128)S(1)}, u32[]{:S(2)}, u32[]{:S(2)}) %collective-permute-start.16) | collective-permute-done | bytes 61472 | tf_op jit(solution)/shard_map/ppermute | solution.py:228
  109.7 3.7 %collective-permute-start.17 = (f32[96,128]{1,0:T(8,128)S(1)}, f32[96,128]{1,0:T(8,128)S(1)}, u32[]{:S(2)}, u32[]{:S(2)}) collective-permute-start(f32[96,128]{1,0:T(8,128)S(1)} %pad_maximum_fusion.11), channel_id=1, source_target_pairs={{0,48},{8,56},{16,32},{24,40},{32,16},{40,24},{48,0},{56,8},{64,11... | collective-permute-start | bytes 147464 | tf_op jit(solution)/shard_map/ppermute | solution.py:228
  113.5 2.6 collective-permute-done.17
  116.2 3.9 %collective-permute-done.18 = f32[72,128]{1,0:T(8,128)S(1)} collective-permute-done((f32[72,128]{1,0:T(8,128)S(1)}, f32[72,128]{1,0:T(8,128)S(1)}, u32[]{:S(2)}, u32[]{:S(2)}) %collective-permute-start.18) | collective-permute-done | bytes 36896 | tf_op jit(solution)/shard_map/ppermute | solution.py:228
  120.2 2.6 collective-permute-start.19
  122.8 2.5 collective-permute-done.19
  125.3 3.2 %operator_round.4 = (f32[144,128]{1,0:T(8,128)S(1)}, f32[12,8,128]{2,1,0:T(8,128)S(1)}, f32[12,8,128]{2,1,0:T(8,128)S(1)}, f32[12,8,128]{2,1,0:T(8,128)S(1)}) custom-call(s32[5,12]{1,0:T(8,128)S(1)} %copy-done.6, f32[24,128]{1,0:T(8,128)S(1)} %get-tuple-element.73.refs_0_, f32[24,128]{1,0:T(8,128)S(1)} %get-tuple-element.87.refs_1_, ...), custom_call_target="tpu_custom_call" | custom-call | tf_op jit(solution)/shard_map/operator_round/pallas_call | solution.py:202
  128.7 4.3 %collective-permute-done.20 = f32[144,128]{1,0:T(8,128)S(1)} collective-permute-done((f32[144,128]{1,0:T(8,128)S(1)}, f32[144,128]{1,0:T(8,128)S(1)}, u32[]{:S(2)}, u32[]{:S(2)}) %collective-permute-start.20) | collective-permute-done | bytes 73760 | tf_op jit(solution)/shard_map/ppermute | solution.py:228
  135.2 3.0 %collective-permute-done.21 = f32[120,128]{1,0:T(8,128)S(1)} collective-permute-done((f32[120,128]{1,0:T(8,128)S(1)}, f32[120,128]{1,0:T(8,128)S(1)}, u32[]{:S(2)}, u32[]{:S(2)}) %collective-permute-start.21) | collective-permute-done | bytes 61472 | tf_op jit(solution)/shard_map/ppermute | solution.py:228
  138.3 3.8 %collective-permute-start.22 = (f32[96,128]{1,0:T(8,128)S(1)}, f32[96,128]{1,0:T(8,128)S(1)}, u32[]{:S(2)}, u32[]{:S(2)}) collective-permute-start(f32[96,128]{1,0:T(8,128)S(1)} %pad_maximum_fusion.12), channel_id=1, source_target_pairs={{0,48},{8,56},{16,32},{24,40},{32,16},{40,24},{48,0},{56,8},{64,11... | collective-permute-start | bytes 147464 | tf_op jit(solution)/shard_map/ppermute | solution.py:228
  142.1 2.5 collective-permute-done.22
  144.7 3.9 %collective-permute-done.23 = f32[72,128]{1,0:T(8,128)S(1)} collective-permute-done((f32[72,128]{1,0:T(8,128)S(1)}, f32[72,128]{1,0:T(8,128)S(1)}, u32[]{:S(2)}, u32[]{:S(2)}) %collective-permute-start.23) | collective-permute-done | bytes 36896 | tf_op jit(solution)/shard_map/ppermute | solution.py:228
  148.7 2.6 collective-permute-start.24
  151.3 2.5 collective-permute-done.24
  153.8 3.2 %precond_round.6 = (f32[144,128]{1,0:T(8,128)S(1)}, f32[12,8,128]{2,1,0:T(8,128)S(1)}, f32[12,8,128]{2,1,0:T(8,128)S(1)}, f32[8,128]{1,0:T(8,128)S(1)}) custom-call(s32[5,12]{1,0:T(8,128)S(1)} %copy-done.6, f32[24,128]{1,0:T(8,128)S(1)} %get-tuple-element.71.refs_0_, f32[24,128]{1,0:T(8,128)S(1)} %get-tuple-element.85.refs_1_, ...), custom_call_target="tpu_custom_call" | custom-call | tf_op jit(solution)/shard_map/precond_round/pallas_call | solution.py:202
  157.2 4.3 %collective-permute-done.25 = f32[144,128]{1,0:T(8,128)S(1)} collective-permute-done((f32[144,128]{1,0:T(8,128)S(1)}, f32[144,128]{1,0:T(8,128)S(1)}, u32[]{:S(2)}, u32[]{:S(2)}) %collective-permute-start.25) | collective-permute-done | bytes 73760 | tf_op jit(solution)/shard_map/ppermute | solution.py:228
  161.5 11.3 %collective-permute-start.26 = (f32[120,128]{1,0:T(8,128)S(1)}, f32[120,128]{1,0:T(8,128)S(1)}, u32[]{:S(2)}, u32[]{:S(2)}) collective-permute-start(f32[120,128]{1,0:T(8,128)S(1)} %pad_maximum_fusion.5), channel_id=1, source_target_pairs={{0,16},{8,24},{16,0},{24,8},{32,48},{40,56},{48,32},{56,40},{64,80... | collective-permute-start | bytes 184328 | tf_op jit(solution)/shard_map/ppermute | solution.py:228
  172.8 3.5 %collective-permute-done.26 = f32[120,128]{1,0:T(8,128)S(1)} collective-permute-done((f32[120,128]{1,0:T(8,128)S(1)}, f32[120,128]{1,0:T(8,128)S(1)}, u32[]{:S(2)}, u32[]{:S(2)}) %collective-permute-start.26) | collective-permute-done | bytes 61472 | tf_op jit(solution)/shard_map/ppermute | solution.py:228
  176.4 3.3 %collective-permute-start.27 = (f32[96,128]{1,0:T(8,128)S(1)}, f32[96,128]{1,0:T(8,128)S(1)}, u32[]{:S(2)}, u32[]{:S(2)}) collective-permute-start(f32[96,128]{1,0:T(8,128)S(1)} %pad_maximum_fusion.13), channel_id=1, source_target_pairs={{0,48},{8,56},{16,32},{24,40},{32,16},{40,24},{48,0},{56,8},{64,11... | collective-permute-start | bytes 147464 | tf_op jit(solution)/shard_map/ppermute | solution.py:228
  179.7 2.9 %collective-permute-done.27 = f32[96,128]{1,0:T(8,128)S(1)} collective-permute-done((f32[96,128]{1,0:T(8,128)S(1)}, f32[96,128]{1,0:T(8,128)S(1)}, u32[]{:S(2)}, u32[]{:S(2)}) %collective-permute-start.27) | collective-permute-done | bytes 49184 | tf_op jit(solution)/shard_map/ppermute | solution.py:228
  182.8 3.9 %collective-permute-done.28 = f32[72,128]{1,0:T(8,128)S(1)} collective-permute-done((f32[72,128]{1,0:T(8,128)S(1)}, f32[72,128]{1,0:T(8,128)S(1)}, u32[]{:S(2)}, u32[]{:S(2)}) %collective-permute-start.28) | collective-permute-done | bytes 36896 | tf_op jit(solution)/shard_map/ppermute | solution.py:228
  186.8 2.4 collective-permute-start.29
  189.2 2.7 %collective-permute-done.29 = f32[48,128]{1,0:T(8,128)S(1)} collective-permute-done((f32[48,128]{1,0:T(8,128)S(1)}, f32[48,128]{1,0:T(8,128)S(1)}, u32[]{:S(2)}, u32[]{:S(2)}) %collective-permute-start.29) | collective-permute-done | bytes 24608 | tf_op jit(solution)/shard_map/ppermute | solution.py:228
  191.9 3.2 %operator_round.5 = (f32[144,128]{1,0:T(8,128)S(1)}, f32[12,8,128]{2,1,0:T(8,128)S(1)}, f32[12,8,128]{2,1,0:T(8,128)}, f32[12,8,128]{2,1,0:T(8,128)S(1)}) custom-call(s32[5,12]{1,0:T(8,128)S(1)} %copy-done.6, f32[24,128]{1,0:T(8,128)S(1)} %get-tuple-element.69.refs_0_, f32[24,128]{1,0:T(8,128)S(1)} %get-tuple-element.83.refs_1_, ...), custom_call_target="tpu_custom_call" | custom-call | tf_op jit(solution)/shard_map/operator_round/pallas_call | solution.py:202
  195.3 4.9 %collective-permute-done.30 = f32[144,128]{1,0:T(8,128)S(1)} collective-permute-done((f32[144,128]{1,0:T(8,128)S(1)}, f32[144,128]{1,0:T(8,128)S(1)}, u32[]{:S(2)}, u32[]{:S(2)}) %collective-permute-start.30) | collective-permute-done | bytes 73760 | tf_op jit(solution)/shard_map/ppermute | solution.py:228
  201.6 3.8 %collective-permute-done.31 = f32[120,128]{1,0:T(8,128)S(1)} collective-permute-done((f32[120,128]{1,0:T(8,128)S(1)}, f32[120,128]{1,0:T(8,128)S(1)}, u32[]{:S(2)}, u32[]{:S(2)}) %collective-permute-start.31) | collective-permute-done | bytes 61472 | tf_op jit(solution)/shard_map/ppermute | solution.py:228
  205.4 3.5 %collective-permute-start.32 = (f32[96,128]{1,0:T(8,128)S(1)}, f32[96,128]{1,0:T(8,128)S(1)}, u32[]{:S(2)}, u32[]{:S(2)}) collective-permute-start(f32[96,128]{1,0:T(8,128)S(1)} %pad_maximum_fusion.14), channel_id=1, source_target_pairs={{0,48},{8,56},{16,32},{24,40},{32,16},{40,24},{48,0},{56,8},{64,11... | collective-permute-start | bytes 147464 | tf_op jit(solution)/shard_map/ppermute | solution.py:228
  208.9 2.8 %collective-permute-done.32 = f32[96,128]{1,0:T(8,128)S(1)} collective-permute-done((f32[96,128]{1,0:T(8,128)S(1)}, f32[96,128]{1,0:T(8,128)S(1)}, u32[]{:S(2)}, u32[]{:S(2)}) %collective-permute-start.32) | collective-permute-done | bytes 49184 | tf_op jit(solution)/shard_map/ppermute | solution.py:228
  211.9 3.9 %collective-permute-done.33 = f32[72,128]{1,0:T(8,128)S(1)} collective-permute-done((f32[72,128]{1,0:T(8,128)S(1)}, f32[72,128]{1,0:T(8,128)S(1)}, u32[]{:S(2)}, u32[]{:S(2)}) %collective-permute-start.33) | collective-permute-done | bytes 36896 | tf_op jit(solution)/shard_map/ppermute | solution.py:228
  215.8 2.5 collective-permute-start.34
  218.3 2.6 collective-permute-done.34
  221.0 3.9 %precond_round.7 = (f32[144,128]{1,0:T(8,128)S(1)}, f32[12,8,128]{2,1,0:T(8,128)}, f32[12,8,128]{2,1,0:T(8,128)S(1)}, f32[8,128]{1,0:T(8,128)S(1)}) custom-call(s32[5,12]{1,0:T(8,128)S(1)} %copy-done.6, f32[24,128]{1,0:T(8,128)S(1)} %get-tuple-element.67.refs_0_, f32[24,128]{1,0:T(8,128)S(1)} %get-tuple-element.81.refs_1_, ...), custom_call_target="tpu_custom_call" | custom-call | tf_op jit(solution)/shard_map/precond_round/pallas_call | solution.py:202
  224.8 4.3 %collective-permute-done.35 = f32[144,128]{1,0:T(8,128)S(1)} collective-permute-done((f32[144,128]{1,0:T(8,128)S(1)}, f32[144,128]{1,0:T(8,128)S(1)}, u32[]{:S(2)}, u32[]{:S(2)}) %collective-permute-start.35) | collective-permute-done | bytes 73760 | tf_op jit(solution)/shard_map/ppermute | solution.py:228
  230.7 3.7 %collective-permute-done.36 = f32[120,128]{1,0:T(8,128)S(1)} collective-permute-done((f32[120,128]{1,0:T(8,128)S(1)}, f32[120,128]{1,0:T(8,128)S(1)}, u32[]{:S(2)}, u32[]{:S(2)}) %collective-permute-start.36) | collective-permute-done | bytes 61472 | tf_op jit(solution)/shard_map/ppermute | solution.py:228
  234.5 4.0 %collective-permute-start.37 = (f32[96,128]{1,0:T(8,128)S(1)}, f32[96,128]{1,0:T(8,128)S(1)}, u32[]{:S(2)}, u32[]{:S(2)}) collective-permute-start(f32[96,128]{1,0:T(8,128)S(1)} %pad_maximum_fusion.15), channel_id=1, source_target_pairs={{0,48},{8,56},{16,32},{24,40},{32,16},{40,24},{48,0},{56,8},{64,11... | collective-permute-start | bytes 147464 | tf_op jit(solution)/shard_map/ppermute | solution.py:228
  240.9 3.9 %collective-permute-done.38 = f32[72,128]{1,0:T(8,128)S(1)} collective-permute-done((f32[72,128]{1,0:T(8,128)S(1)}, f32[72,128]{1,0:T(8,128)S(1)}, u32[]{:S(2)}, u32[]{:S(2)}) %collective-permute-start.38) | collective-permute-done | bytes 36896 | tf_op jit(solution)/shard_map/ppermute | solution.py:228
  244.9 2.6 collective-permute-start.39
  247.5 2.5 collective-permute-done.39
  255.1 2.9 %collective-permute-done.41 = f32[128,128]{1,0:T(8,128)S(1)} collective-permute-done((f32[128,128]{1,0:T(8,128)S(1)}, f32[128,128]{1,0:T(8,128)S(1)}, u32[]{:S(2)}, u32[]{:S(2)}) %collective-permute-start.41) | collective-permute-done | bytes 65568 | tf_op jit(solution)/shard_map/ppermute | solution.py:298
  258.1 2.9 %collective-permute-start.42 = (f32[128,128]{1,0:T(8,128)S(1)}, f32[128,128]{1,0:T(8,128)S(1)}, u32[]{:S(2)}, u32[]{:S(2)}) collective-permute-start(f32[128,128]{1,0:T(8,128)S(1)} %add.353), channel_id=1, source_target_pairs={{0,6},{1,7},{2,4},{3,5},{4,2},{5,3},{6,0},{7,1},{8,14},{9,15},{10,... | collective-permute-start | bytes 196616 | tf_op jit(solution)/shard_map/ppermute | solution.py:298
  (200 shorter events, 40.3 us)
Async XLA Ops:
  0.6 2.1 copy-start.3
  2.7 2.6 copy-start.4
  2.8 3.6 %copy-start.9 = (f32[1,1536]{1,0:T(1,128)S(1)}, f32[1,1536]{1,0:T(1,128)}, u32[]{:S(2)}) copy-start(f32[1,1536]{1,0:T(1,128)} %param.8) | copy-start | bytes 18436
  2.8 3.7 %copy-start.8 = (f32[1536]{0:T(1024)S(1)}, f32[1536]{0:T(1024)}, u32[]{:S(2)}) copy-start(f32[1536]{0:T(1024)} %param.10) | copy-start | bytes 18436
  2.8 3.7 %copy-start.6 = (s32[5,12]{1,0:T(8,128)S(1)}, s32[5,12]{1,0:T(8,128)}, u32[]{:S(2)}) copy-start(s32[5,12]{1,0:T(8,128)} %sep.15) | copy-start | bytes 724
  3.5 1.9 copy-start
  5.4 31.0 %copy-start.5 = (f32[12,128,128]{2,1,0:T(8,128)S(1)}, f32[12,128,128]{2,1,0:T(8,128)}, u32[]{:S(2)}) copy-start(f32[12,128,128]{2,1,0:T(8,128)} %mat_ref.3) | copy-start | bytes 2359300
  6.4 2.1 copy-start.1
  8.5 30.2 %copy-start.2 = (bf16[60,256,128]{2,1,0:T(8,128)(2,1)S(1)}, bf16[60,256,128]{2,1,0:T(8,128)(2,1)}, u32[]{:S(2)}) copy-start(bf16[60,256,128]{2,1,0:T(8,128)(2,1)} %copy-done) | copy-start | bytes 11796484
  11.1 4.4 %collective-permute-start = (f32[144,128]{1,0:T(8,128)S(1)}, f32[144,128]{1,0:T(8,128)S(1)}, u32[]{:S(2)}, u32[]{:S(2)}) collective-permute-start(f32[144,128]{1,0:T(8,128)S(1)} %get-tuple-element.32), channel_id=1, source_target_pairs={{0,8},{8,0},{16,24},{24,16},{32,40},{40,32},{48,56},{56,48},{64,72... | collective-permute-start | bytes 221192 | tf_op jit(solution)/shard_map/ppermute | solution.py:228
  15.5 5.6 %collective-permute-start.1 = (f32[120,128]{1,0:T(8,128)S(1)}, f32[120,128]{1,0:T(8,128)S(1)}, u32[]{:S(2)}, u32[]{:S(2)}) collective-permute-start(f32[120,128]{1,0:T(8,128)S(1)} %pad_maximum_fusion), channel_id=1, source_target_pairs={{0,16},{8,24},{16,0},{24,8},{32,48},{40,56},{48,32},{56,40},{64,80... | collective-permute-start | bytes 184328 | tf_op jit(solution)/shard_map/ppermute | solution.py:228
  21.2 8.3 %collective-permute-start.2 = (f32[96,128]{1,0:T(8,128)S(1)}, f32[96,128]{1,0:T(8,128)S(1)}, u32[]{:S(2)}, u32[]{:S(2)}) collective-permute-start(f32[96,128]{1,0:T(8,128)S(1)} %pad_maximum_fusion.8), channel_id=1, source_target_pairs={{0,48},{8,56},{16,32},{24,40},{32,16},{40,24},{48,0},{56,8},{64,11... | collective-permute-start | bytes 147464 | tf_op jit(solution)/shard_map/ppermute | solution.py:228
  29.6 4.0 %collective-permute-start.3 = (f32[72,128]{1,0:T(8,128)S(1)}, f32[72,128]{1,0:T(8,128)S(1)}, u32[]{:S(2)}, u32[]{:S(2)}) collective-permute-start(f32[72,128]{1,0:T(8,128)S(1)} %pad_maximum_fusion.16), channel_id=1, source_target_pairs={{0,64},{8,72},{16,80},{24,88},{32,96},{40,104},{48,112},{56,120},{... | collective-permute-start | bytes 110600 | tf_op jit(solution)/shard_map/ppermute | solution.py:228
  33.6 5.1 %collective-permute-start.4 = (f32[48,128]{1,0:T(8,128)S(1)}, f32[48,128]{1,0:T(8,128)S(1)}, u32[]{:S(2)}, u32[]{:S(2)}) collective-permute-start(f32[48,128]{1,0:T(8,128)S(1)} %pad_maximum_fusion.24), channel_id=1, source_target_pairs={{0,192},{8,200},{16,208},{24,216},{32,224},{40,232},{48,240},{56,2... | collective-permute-start | bytes 73736 | tf_op jit(solution)/shard_map/ppermute | solution.py:228
  42.0 4.4 %collective-permute-start.5 = (f32[144,128]{1,0:T(8,128)S(1)}, f32[144,128]{1,0:T(8,128)S(1)}, u32[]{:S(2)}, u32[]{:S(2)}) collective-permute-start(f32[144,128]{1,0:T(8,128)S(1)} %get-tuple-element.34), channel_id=1, source_target_pairs={{0,8},{8,0},{16,24},{24,16},{32,40},{40,32},{48,56},{56,48},{64,72... | collective-permute-start | bytes 221192 | tf_op jit(solution)/shard_map/ppermute | solution.py:228
  46.5 5.2 %collective-permute-start.6 = (f32[120,128]{1,0:T(8,128)S(1)}, f32[120,128]{1,0:T(8,128)S(1)}, u32[]{:S(2)}, u32[]{:S(2)}) collective-permute-start(f32[120,128]{1,0:T(8,128)S(1)} %pad_maximum_fusion.1), channel_id=1, source_target_pairs={{0,16},{8,24},{16,0},{24,8},{32,48},{40,56},{48,32},{56,40},{64,80... | collective-permute-start | bytes 184328 | tf_op jit(solution)/shard_map/ppermute | solution.py:228
  51.7 6.4 %collective-permute-start.7 = (f32[96,128]{1,0:T(8,128)S(1)}, f32[96,128]{1,0:T(8,128)S(1)}, u32[]{:S(2)}, u32[]{:S(2)}) collective-permute-start(f32[96,128]{1,0:T(8,128)S(1)} %pad_maximum_fusion.9), channel_id=1, source_target_pairs={{0,48},{8,56},{16,32},{24,40},{32,16},{40,24},{48,0},{56,8},{64,11... | collective-permute-start | bytes 147464 | tf_op jit(solution)/shard_map/ppermute | solution.py:228
  58.2 4.0 %collective-permute-start.8 = (f32[72,128]{1,0:T(8,128)S(1)}, f32[72,128]{1,0:T(8,128)S(1)}, u32[]{:S(2)}, u32[]{:S(2)}) collective-permute-start(f32[72,128]{1,0:T(8,128)S(1)} %pad_maximum_fusion.17), channel_id=1, source_target_pairs={{0,64},{8,72},{16,80},{24,88},{32,96},{40,104},{48,112},{56,120},{... | collective-permute-start | bytes 110600 | tf_op jit(solution)/shard_map/ppermute | solution.py:228
  62.3 5.1 %collective-permute-start.9 = (f32[48,128]{1,0:T(8,128)S(1)}, f32[48,128]{1,0:T(8,128)S(1)}, u32[]{:S(2)}, u32[]{:S(2)}) collective-permute-start(f32[48,128]{1,0:T(8,128)S(1)} %pad_maximum_fusion.25), channel_id=1, source_target_pairs={{0,192},{8,200},{16,208},{24,216},{32,224},{40,232},{48,240},{56,2... | collective-permute-start | bytes 73736 | tf_op jit(solution)/shard_map/ppermute | solution.py:228
  70.6 4.4 %collective-permute-start.10 = (f32[144,128]{1,0:T(8,128)S(1)}, f32[144,128]{1,0:T(8,128)S(1)}, u32[]{:S(2)}, u32[]{:S(2)}) collective-permute-start(f32[144,128]{1,0:T(8,128)S(1)} %get-tuple-element.38), channel_id=1, source_target_pairs={{0,8},{8,0},{16,24},{24,16},{32,40},{40,32},{48,56},{56,48},{64,72... | collective-permute-start | bytes 221192 | tf_op jit(solution)/shard_map/ppermute | solution.py:228
  75.1 5.2 %collective-permute-start.11 = (f32[120,128]{1,0:T(8,128)S(1)}, f32[120,128]{1,0:T(8,128)S(1)}, u32[]{:S(2)}, u32[]{:S(2)}) collective-permute-start(f32[120,128]{1,0:T(8,128)S(1)} %pad_maximum_fusion.2), channel_id=1, source_target_pairs={{0,16},{8,24},{16,0},{24,8},{32,48},{40,56},{48,32},{56,40},{64,80... | collective-permute-start | bytes 184328 | tf_op jit(solution)/shard_map/ppermute | solution.py:228
  80.4 7.1 %collective-permute-start.12 = (f32[96,128]{1,0:T(8,128)S(1)}, f32[96,128]{1,0:T(8,128)S(1)}, u32[]{:S(2)}, u32[]{:S(2)}) collective-permute-start(f32[96,128]{1,0:T(8,128)S(1)} %pad_maximum_fusion.10), channel_id=1, source_target_pairs={{0,48},{8,56},{16,32},{24,40},{32,16},{40,24},{48,0},{56,8},{64,11... | collective-permute-start | bytes 147464 | tf_op jit(solution)/shard_map/ppermute | solution.py:228
  87.5 4.0 %collective-permute-start.13 = (f32[72,128]{1,0:T(8,128)S(1)}, f32[72,128]{1,0:T(8,128)S(1)}, u32[]{:S(2)}, u32[]{:S(2)}) collective-permute-start(f32[72,128]{1,0:T(8,128)S(1)} %pad_maximum_fusion.18), channel_id=1, source_target_pairs={{0,64},{8,72},{16,80},{24,88},{32,96},{40,104},{48,112},{56,120},{... | collective-permute-start | bytes 110600 | tf_op jit(solution)/shard_map/ppermute | solution.py:228
  91.6 5.1 %collective-permute-start.14 = (f32[48,128]{1,0:T(8,128)S(1)}, f32[48,128]{1,0:T(8,128)S(1)}, u32[]{:S(2)}, u32[]{:S(2)}) collective-permute-start(f32[48,128]{1,0:T(8,128)S(1)} %pad_maximum_fusion.26), channel_id=1, source_target_pairs={{0,192},{8,200},{16,208},{24,216},{32,224},{40,232},{48,240},{56,2... | collective-permute-start | bytes 73736 | tf_op jit(solution)/shard_map/ppermute | solution.py:228
  100.0 4.4 %collective-permute-start.15 = (f32[144,128]{1,0:T(8,128)S(1)}, f32[144,128]{1,0:T(8,128)S(1)}, u32[]{:S(2)}, u32[]{:S(2)}) collective-permute-start(f32[144,128]{1,0:T(8,128)S(1)} %get-tuple-element.40), channel_id=1, source_target_pairs={{0,8},{8,0},{16,24},{24,16},{32,40},{40,32},{48,56},{56,48},{64,72... | collective-permute-start | bytes 221192 | tf_op jit(solution)/shard_map/ppermute | solution.py:228
  104.4 5.2 %collective-permute-start.16 = (f32[120,128]{1,0:T(8,128)S(1)}, f32[120,128]{1,0:T(8,128)S(1)}, u32[]{:S(2)}, u32[]{:S(2)}) collective-permute-start(f32[120,128]{1,0:T(8,128)S(1)} %pad_maximum_fusion.3), channel_id=1, source_target_pairs={{0,16},{8,24},{16,0},{24,8},{32,48},{40,56},{48,32},{56,40},{64,80... | collective-permute-start | bytes 184328 | tf_op jit(solution)/shard_map/ppermute | solution.py:228
  109.7 6.3 %collective-permute-start.17 = (f32[96,128]{1,0:T(8,128)S(1)}, f32[96,128]{1,0:T(8,128)S(1)}, u32[]{:S(2)}, u32[]{:S(2)}) collective-permute-start(f32[96,128]{1,0:T(8,128)S(1)} %pad_maximum_fusion.11), channel_id=1, source_target_pairs={{0,48},{8,56},{16,32},{24,40},{32,16},{40,24},{48,0},{56,8},{64,11... | collective-permute-start | bytes 147464 | tf_op jit(solution)/shard_map/ppermute | solution.py:228
  116.1 4.0 %collective-permute-start.18 = (f32[72,128]{1,0:T(8,128)S(1)}, f32[72,128]{1,0:T(8,128)S(1)}, u32[]{:S(2)}, u32[]{:S(2)}) collective-permute-start(f32[72,128]{1,0:T(8,128)S(1)} %pad_maximum_fusion.19), channel_id=1, source_target_pairs={{0,64},{8,72},{16,80},{24,88},{32,96},{40,104},{48,112},{56,120},{... | collective-permute-start | bytes 110600 | tf_op jit(solution)/shard_map/ppermute | solution.py:228
  120.2 5.1 %collective-permute-start.19 = (f32[48,128]{1,0:T(8,128)S(1)}, f32[48,128]{1,0:T(8,128)S(1)}, u32[]{:S(2)}, u32[]{:S(2)}) collective-permute-start(f32[48,128]{1,0:T(8,128)S(1)} %pad_maximum_fusion.27), channel_id=1, source_target_pairs={{0,192},{8,200},{16,208},{24,216},{32,224},{40,232},{48,240},{56,2... | collective-permute-start | bytes 73736 | tf_op jit(solution)/shard_map/ppermute | solution.py:228
  128.5 4.4 %collective-permute-start.20 = (f32[144,128]{1,0:T(8,128)S(1)}, f32[144,128]{1,0:T(8,128)S(1)}, u32[]{:S(2)}, u32[]{:S(2)}) collective-permute-start(f32[144,128]{1,0:T(8,128)S(1)} %get-tuple-element.46), channel_id=1, source_target_pairs={{0,8},{8,0},{16,24},{24,16},{32,40},{40,32},{48,56},{56,48},{64,72... | collective-permute-start | bytes 221192 | tf_op jit(solution)/shard_map/ppermute | solution.py:228
  133.0 5.2 %collective-permute-start.21 = (f32[120,128]{1,0:T(8,128)S(1)}, f32[120,128]{1,0:T(8,128)S(1)}, u32[]{:S(2)}, u32[]{:S(2)}) collective-permute-start(f32[120,128]{1,0:T(8,128)S(1)} %pad_maximum_fusion.4), channel_id=1, source_target_pairs={{0,16},{8,24},{16,0},{24,8},{32,48},{40,56},{48,32},{56,40},{64,80... | collective-permute-start | bytes 184328 | tf_op jit(solution)/shard_map/ppermute | solution.py:228
  138.3 6.3 %collective-permute-start.22 = (f32[96,128]{1,0:T(8,128)S(1)}, f32[96,128]{1,0:T(8,128)S(1)}, u32[]{:S(2)}, u32[]{:S(2)}) collective-permute-start(f32[96,128]{1,0:T(8,128)S(1)} %pad_maximum_fusion.12), channel_id=1, source_target_pairs={{0,48},{8,56},{16,32},{24,40},{32,16},{40,24},{48,0},{56,8},{64,11... | collective-permute-start | bytes 147464 | tf_op jit(solution)/shard_map/ppermute | solution.py:228
  144.6 4.0 %collective-permute-start.23 = (f32[72,128]{1,0:T(8,128)S(1)}, f32[72,128]{1,0:T(8,128)S(1)}, u32[]{:S(2)}, u32[]{:S(2)}) collective-permute-start(f32[72,128]{1,0:T(8,128)S(1)} %pad_maximum_fusion.20), channel_id=1, source_target_pairs={{0,64},{8,72},{16,80},{24,88},{32,96},{40,104},{48,112},{56,120},{... | collective-permute-start | bytes 110600 | tf_op jit(solution)/shard_map/ppermute | solution.py:228
  148.7 5.1 %collective-permute-start.24 = (f32[48,128]{1,0:T(8,128)S(1)}, f32[48,128]{1,0:T(8,128)S(1)}, u32[]{:S(2)}, u32[]{:S(2)}) collective-permute-start(f32[48,128]{1,0:T(8,128)S(1)} %pad_maximum_fusion.28), channel_id=1, source_target_pairs={{0,192},{8,200},{16,208},{24,216},{32,224},{40,232},{48,240},{56,2... | collective-permute-start | bytes 73736 | tf_op jit(solution)/shard_map/ppermute | solution.py:228
  157.1 4.4 %collective-permute-start.25 = (f32[144,128]{1,0:T(8,128)S(1)}, f32[144,128]{1,0:T(8,128)S(1)}, u32[]{:S(2)}, u32[]{:S(2)}) collective-permute-start(f32[144,128]{1,0:T(8,128)S(1)} %get-tuple-element.48), channel_id=1, source_target_pairs={{0,8},{8,0},{16,24},{24,16},{32,40},{40,32},{48,56},{56,48},{64,72... | collective-permute-start | bytes 221192 | tf_op jit(solution)/shard_map/ppermute | solution.py:228
  161.5 14.8 %collective-permute-start.26 = (f32[120,128]{1,0:T(8,128)S(1)}, f32[120,128]{1,0:T(8,128)S(1)}, u32[]{:S(2)}, u32[]{:S(2)}) collective-permute-start(f32[120,128]{1,0:T(8,128)S(1)} %pad_maximum_fusion.5), channel_id=1, source_target_pairs={{0,16},{8,24},{16,0},{24,8},{32,48},{40,56},{48,32},{56,40},{64,80... | collective-permute-start | bytes 184328 | tf_op jit(solution)/shard_map/ppermute | solution.py:228
  176.4 6.3 %collective-permute-start.27 = (f32[96,128]{1,0:T(8,128)S(1)}, f32[96,128]{1,0:T(8,128)S(1)}, u32[]{:S(2)}, u32[]{:S(2)}) collective-permute-start(f32[96,128]{1,0:T(8,128)S(1)} %pad_maximum_fusion.13), channel_id=1, source_target_pairs={{0,48},{8,56},{16,32},{24,40},{32,16},{40,24},{48,0},{56,8},{64,11... | collective-permute-start | bytes 147464 | tf_op jit(solution)/shard_map/ppermute | solution.py:228
  182.7 4.0 %collective-permute-start.28 = (f32[72,128]{1,0:T(8,128)S(1)}, f32[72,128]{1,0:T(8,128)S(1)}, u32[]{:S(2)}, u32[]{:S(2)}) collective-permute-start(f32[72,128]{1,0:T(8,128)S(1)} %pad_maximum_fusion.21), channel_id=1, source_target_pairs={{0,64},{8,72},{16,80},{24,88},{32,96},{40,104},{48,112},{56,120},{... | collective-permute-start | bytes 110600 | tf_op jit(solution)/shard_map/ppermute | solution.py:228
  186.8 5.1 %collective-permute-start.29 = (f32[48,128]{1,0:T(8,128)S(1)}, f32[48,128]{1,0:T(8,128)S(1)}, u32[]{:S(2)}, u32[]{:S(2)}) collective-permute-start(f32[48,128]{1,0:T(8,128)S(1)} %pad_maximum_fusion.29), channel_id=1, source_target_pairs={{0,192},{8,200},{16,208},{24,216},{32,224},{40,232},{48,240},{56,2... | collective-permute-start | bytes 73736 | tf_op jit(solution)/shard_map/ppermute | solution.py:228
  195.1 52.4 %copy-start.7 = (s32[2,16384]{1,0:T(2,128)S(1)}, s32[2,16384]{1,0:T(2,128)}, u32[]{:S(2)}) copy-start(s32[2,16384]{1,0:T(2,128)} %param.15) | copy-start | bytes 393220
  195.2 5.0 %collective-permute-start.30 = (f32[144,128]{1,0:T(8,128)S(1)}, f32[144,128]{1,0:T(8,128)S(1)}, u32[]{:S(2)}, u32[]{:S(2)}) collective-permute-start(f32[144,128]{1,0:T(8,128)S(1)} %get-tuple-element.54), channel_id=1, source_target_pairs={{0,8},{8,0},{16,24},{24,16},{32,40},{40,32},{48,56},{56,48},{64,72... | collective-permute-start | bytes 221192 | tf_op jit(solution)/shard_map/ppermute | solution.py:228
  200.2 5.2 %collective-permute-start.31 = (f32[120,128]{1,0:T(8,128)S(1)}, f32[120,128]{1,0:T(8,128)S(1)}, u32[]{:S(2)}, u32[]{:S(2)}) collective-permute-start(f32[120,128]{1,0:T(8,128)S(1)} %pad_maximum_fusion.6), channel_id=1, source_target_pairs={{0,16},{8,24},{16,0},{24,8},{32,48},{40,56},{48,32},{56,40},{64,80... | collective-permute-start | bytes 184328 | tf_op jit(solution)/shard_map/ppermute | solution.py:228
  205.4 6.3 %collective-permute-start.32 = (f32[96,128]{1,0:T(8,128)S(1)}, f32[96,128]{1,0:T(8,128)S(1)}, u32[]{:S(2)}, u32[]{:S(2)}) collective-permute-start(f32[96,128]{1,0:T(8,128)S(1)} %pad_maximum_fusion.14), channel_id=1, source_target_pairs={{0,48},{8,56},{16,32},{24,40},{32,16},{40,24},{48,0},{56,8},{64,11... | collective-permute-start | bytes 147464 | tf_op jit(solution)/shard_map/ppermute | solution.py:228
  211.8 4.0 %collective-permute-start.33 = (f32[72,128]{1,0:T(8,128)S(1)}, f32[72,128]{1,0:T(8,128)S(1)}, u32[]{:S(2)}, u32[]{:S(2)}) collective-permute-start(f32[72,128]{1,0:T(8,128)S(1)} %pad_maximum_fusion.22), channel_id=1, source_target_pairs={{0,64},{8,72},{16,80},{24,88},{32,96},{40,104},{48,112},{56,120},{... | collective-permute-start | bytes 110600 | tf_op jit(solution)/shard_map/ppermute | solution.py:228
  215.8 5.1 %collective-permute-start.34 = (f32[48,128]{1,0:T(8,128)S(1)}, f32[48,128]{1,0:T(8,128)S(1)}, u32[]{:S(2)}, u32[]{:S(2)}) collective-permute-start(f32[48,128]{1,0:T(8,128)S(1)} %pad_maximum_fusion.30), channel_id=1, source_target_pairs={{0,192},{8,200},{16,208},{24,216},{32,224},{40,232},{48,240},{56,2... | collective-permute-start | bytes 73736 | tf_op jit(solution)/shard_map/ppermute | solution.py:228
  224.8 4.4 %collective-permute-start.35 = (f32[144,128]{1,0:T(8,128)S(1)}, f32[144,128]{1,0:T(8,128)S(1)}, u32[]{:S(2)}, u32[]{:S(2)}) collective-permute-start(f32[144,128]{1,0:T(8,128)S(1)} %get-tuple-element.56), channel_id=1, source_target_pairs={{0,8},{8,0},{16,24},{24,16},{32,40},{40,32},{48,56},{56,48},{64,72... | collective-permute-start | bytes 221192 | tf_op jit(solution)/shard_map/ppermute | solution.py:228
  229.2 5.2 %collective-permute-start.36 = (f32[120,128]{1,0:T(8,128)S(1)}, f32[120,128]{1,0:T(8,128)S(1)}, u32[]{:S(2)}, u32[]{:S(2)}) collective-permute-start(f32[120,128]{1,0:T(8,128)S(1)} %pad_maximum_fusion.7), channel_id=1, source_target_pairs={{0,16},{8,24},{16,0},{24,8},{32,48},{40,56},{48,32},{56,40},{64,80... | collective-permute-start | bytes 184328 | tf_op jit(solution)/shard_map/ppermute | solution.py:228
  234.5 6.3 %collective-permute-start.37 = (f32[96,128]{1,0:T(8,128)S(1)}, f32[96,128]{1,0:T(8,128)S(1)}, u32[]{:S(2)}, u32[]{:S(2)}) collective-permute-start(f32[96,128]{1,0:T(8,128)S(1)} %pad_maximum_fusion.15), channel_id=1, source_target_pairs={{0,48},{8,56},{16,32},{24,40},{32,16},{40,24},{48,0},{56,8},{64,11... | collective-permute-start | bytes 147464 | tf_op jit(solution)/shard_map/ppermute | solution.py:228
  240.8 4.0 %collective-permute-start.38 = (f32[72,128]{1,0:T(8,128)S(1)}, f32[72,128]{1,0:T(8,128)S(1)}, u32[]{:S(2)}, u32[]{:S(2)}) collective-permute-start(f32[72,128]{1,0:T(8,128)S(1)} %pad_maximum_fusion.23), channel_id=1, source_target_pairs={{0,64},{8,72},{16,80},{24,88},{32,96},{40,104},{48,112},{56,120},{... | collective-permute-start | bytes 110600 | tf_op jit(solution)/shard_map/ppermute | solution.py:228
  244.9 5.1 %collective-permute-start.39 = (f32[48,128]{1,0:T(8,128)S(1)}, f32[48,128]{1,0:T(8,128)S(1)}, u32[]{:S(2)}, u32[]{:S(2)}) collective-permute-start(f32[48,128]{1,0:T(8,128)S(1)} %pad_maximum_fusion.31), channel_id=1, source_target_pairs={{0,192},{8,200},{16,208},{24,216},{32,224},{40,232},{48,240},{56,2... | collective-permute-start | bytes 73736 | tf_op jit(solution)/shard_map/ppermute | solution.py:228
  252.3 1.3 collective-permute-start.40
  253.7 4.4 %collective-permute-start.41 = (f32[128,128]{1,0:T(8,128)S(1)}, f32[128,128]{1,0:T(8,128)S(1)}, u32[]{:S(2)}, u32[]{:S(2)}) collective-permute-start(f32[128,128]{1,0:T(8,128)S(1)} %add.352), channel_id=1, source_target_pairs={{0,2},{1,3},{2,0},{3,1},{4,6},{5,7},{6,4},{7,5},{8,10},{9,11},{10,... | collective-permute-start | bytes 196616 | tf_op jit(solution)/shard_map/ppermute | solution.py:298
  258.1 5.6 %collective-permute-start.42 = (f32[128,128]{1,0:T(8,128)S(1)}, f32[128,128]{1,0:T(8,128)S(1)}, u32[]{:S(2)}, u32[]{:S(2)}) collective-permute-start(f32[128,128]{1,0:T(8,128)S(1)} %add.353), channel_id=1, source_target_pairs={{0,6},{1,7},{2,4},{3,5},{4,2},{5,3},{6,0},{7,1},{8,14},{9,15},{10,... | collective-permute-start | bytes 196616 | tf_op jit(solution)/shard_map/ppermute | solution.py:298
